TPU v7x, 256 devices: a whole 4x4x8 slice. The times are simulated.
256 devices in a mesh: row: 8 (over x, core), col: 32 (over z, y).
Axes of the slice: x: 4, y: 4, z: 8, core: 2. Of those that a mesh axis runs over, the one named last changes fastest.
Arguments:
- layer_input: bfloat16 [16896, 1024], P('col', 'row'), may hold values from -6 to 6
- w_q: bfloat16 [1024, 1024], P('col', 'row'), may hold values from -0.1875 to 0.1875
- w_k: bfloat16 [1024, 1024], P('col', 'row'), may hold values from -0.1875 to 0.1875
- w_v: bfloat16 [1024, 1024], P('col', 'row'), may hold values from -0.1875 to 0.1875
- w_o: bfloat16 [1024, 1024], P('row', 'col'), may hold values from -0.375 to 0.375
- w_gate: bfloat16 [1024, 4096], P('col', 'row'), may hold values from -0.1875 to 0.1875
- w_up: bfloat16 [1024, 4096], P('col', 'row'), may hold values from -0.1875 to 0.1875
- w_down: bfloat16 [4096, 1024], P('row', 'col'), may hold values from -0.1875 to 0.1875
- norm1: float32 [1024], replicated, may hold values from 0.5 to 1.5
- norm2: float32 [1024], replicated, may hold values from 0.5 to 1.5
- q_gain: float32 [1024], P('row'), may hold values from 0.5 to 1.5
- k_gain: float32 [1024], P('row'), may hold values from 0.5 to 1.5
- bias_same: float32 [16], P('row'), may hold values from -3 to 3
- bias_diff: float32 [16], P('row'), may hold values from -3 to 3
- pre_variate: int32 [32, 512], P('col'), may hold values from 0 to 7, never falling along the last dimension, each value on 1 to 128 neighbouring positions
- pre_keep: int32 [32, 512], P('col'), may hold values 0 or 1
- dec_variate: int32 [512], P('col'), may hold values from 0 to 7
- dec_len: int32 [512], P('col'), may hold values from 1 to 1023, as said below
- dec_table: int32 [512, 8], P('col'), may hold values from 0 to 31
- dec_holder: int32 [512, 1], P('col'), may hold values from 0 to 31; in each aligned block of 16 rows (0 to 15, 16 to 31, ...) at most 2 rows name the same one
- kv_pool: bfloat16 [1024, 2, 128, 1024], P('col', None, None, 'row'), may hold values from -4 to 4
- page_variates: int32 [1024, 128], P('col'), may hold values from 0 to 7
Outputs:
- hidden: bfloat16 [16896, 1024], P('col', 'row')
- prefill_pages: bfloat16 [128, 2, 128, 1024], P('col', None, None, 'row')
- tail_pages: bfloat16 [512, 2, 128, 1024], P('col', None, None, 'row')
Inputs may be any that keep to these rules, and one draw needn't show every extreme that they name: `pre_variate`: each variate's tokens form one run of at most 128 positions. `dec_len`: some request has exactly 1023 cached tokens. `dec_table`: entries past a request's last page are unused; requests may share pages. `dec_holder`: among the 16 requests of one column group at most 2 name the same holder, a bound that some block reaches of them.
All inputs are finite; a program needn't handle non-finite values. No bound on the sum of `pre_keep` on one device may be relied on, other than what follows from the above.
Results may differ from a plain program's by a relative error of at most 0.015.
Values may be sent and summed in bfloat16 or wider, within the bound.
No kernel may reach another device: no remote copies, remote signals or barrier semaphores. Data moves between devices by JAX's collectives and lax.ppermute only.
A program may use at most 128 MiB of HBM per device.

v0:
```python
import jax
import jax.numpy as jnp
from jax import lax
from jax.sharding import PartitionSpec as P

HD = 64
eps = 1e-05


def as_sent(array):
    return jax.tree.map(lambda a: a.astype(jnp.bfloat16) if a.dtype == jnp.float32 else a, array)


def norm_rows(values, gain_row):
    return values * lax.rsqrt(jnp.mean(values * values, axis=-1, keepdims=True) + eps) * gain_row


def rotate(tensor, places):
    half_size = tensor.shape[-1] // 2
    spacing = jnp.arange(half_size).astype(jnp.float32) * (2.0 / tensor.shape[-1])
    angles = places.astype(jnp.float32)[:, None] * jnp.power(10000.0, -spacing)[None, :]
    cosine = jnp.cos(angles)[:, None, :]
    sine_part = jnp.sin(angles)[:, None, :]
    lower_half = tensor[..., :half_size]
    upper_half = tensor[..., half_size:]
    return jnp.concatenate(
        [
            lower_half * cosine - upper_half * sine_part,
            upper_half * cosine + lower_half * sine_part,
        ],
        axis=-1,
    )


def segment_time(variates):
    places = jnp.arange(variates.shape[0])
    run_start = jnp.concatenate([jnp.ones((1,), dtype=jnp.bool_), variates[1:] != variates[:-1]])
    starts = lax.cummax(jnp.where(run_start, places, 0), axis=0)
    return places - starts


def on_device(
    layer_input,
    w_q,
    w_k,
    w_v,
    w_o,
    w_gate,
    w_up,
    w_down,
    norm1,
    norm2,
    q_gain,
    k_gain,
    bias_same,
    bias_diff,
    pre_variate,
    pre_keep,
    dec_variate,
    dec_len,
    dec_table,
    dec_holder,
    kv_pool,
    page_variates,
):
    row_count = layer_input.shape[0]
    local_width = layer_input.shape[1]
    pre_len = pre_variate.shape[1]
    dec_count = dec_len.shape[0]
    heads_here = local_width // HD
    score_scale = HD ** (-0.5)
    page_size = kv_pool.shape[2]
    page_count = dec_table.shape[1]
    gathered_input = lax.all_gather(layer_input, "row", axis=1, tiled=True)
    normed = norm_rows(gathered_input.astype(jnp.float32), norm1).astype(jnp.bfloat16)
    pieces = (
        lax.all_gather(w_q, "col", axis=0, tiled=True),
        lax.all_gather(w_k, "col", axis=0, tiled=True),
        lax.all_gather(w_v, "col", axis=0, tiled=True),
    )
    columns = normed
    queries = jnp.dot(columns, pieces[0], preferred_element_type=jnp.float32)
    keys_proj = jnp.dot(columns, pieces[1], preferred_element_type=jnp.float32)
    values_proj = jnp.dot(columns, pieces[2], preferred_element_type=jnp.float32)
    places = jnp.concatenate([segment_time(pre_variate[0]), dec_len])
    query_rot = rotate(
        norm_rows(queries.reshape(row_count, heads_here, HD), q_gain.reshape(heads_here, HD)),
        places,
    ).astype(jnp.bfloat16)
    key_rot = rotate(
        norm_rows(keys_proj.reshape(row_count, heads_here, HD), k_gain.reshape(heads_here, HD)),
        places,
    ).astype(jnp.bfloat16)
    value_bf = values_proj.astype(jnp.bfloat16).reshape(row_count, heads_here, HD)

    def attend_slot(inputs):
        float_item, int_item = inputs
        new_query = float_item[:local_width].reshape(heads_here, HD)
        new_key = float_item[local_width : 2 * local_width]
        new_value = float_item[2 * local_width :]
        page_rows = int_item[:page_count]
        length = int_item[page_count]
        variate = int_item[page_count + 1]
        gathered = kv_pool[page_rows]
        cached_keys = gathered[:, 0].reshape(page_count * page_size, heads_here, HD)
        cached_vals = gathered[:, 1].reshape(page_count * page_size, heads_here, HD)
        key_variates = page_variates[page_rows].reshape(page_count * page_size)
        scores = (
            jnp.einsum("hd,khd->hk", new_query, cached_keys, preferred_element_type=jnp.float32)
            * score_scale
        )
        scores = scores + jnp.where(
            (key_variates == variate)[None, :], bias_same[:, None], bias_diff[:, None]
        )
        key_heads = new_key.reshape(heads_here, HD)
        value_heads = new_value.reshape(heads_here, HD)
        own_score = (
            jnp.sum(new_query.astype(jnp.float32) * key_heads.astype(jnp.float32), axis=1)
            * score_scale
            + bias_same
        )
        exp_scores = jnp.where(
            (jnp.arange(page_count * page_size) < length)[None, :], jnp.exp(scores), 0.0
        )
        own_exp = jnp.exp(own_score)
        total_weight = jnp.sum(exp_scores, axis=1) + own_exp
        weights_bf = (exp_scores / total_weight[:, None]).astype(jnp.bfloat16)
        own_weight = (own_exp / total_weight).astype(jnp.bfloat16)
        attended = jnp.einsum(
            "hk,khd->hd", weights_bf, cached_vals, preferred_element_type=jnp.float32
        ) + own_weight.astype(jnp.float32)[:, None] * value_heads.astype(jnp.float32)
        tail_slot = page_rows[length // page_size]
        old_page = kv_pool[tail_slot]
        hit_row = (jnp.arange(page_size) == length % page_size)[None, :, None]
        new_rows = jnp.stack([new_key, new_value])[:, None, :]
        return (
            attended.astype(jnp.bfloat16).reshape(local_width),
            jnp.where(hit_row, new_rows, old_page),
        )

    keep_mask = pre_keep[0]
    variates = pre_variate[0]
    block_rows = min(512, pre_len)
    pre_keys = key_rot[:pre_len]
    pre_values = value_bf[:pre_len]
    block_queries = query_rot[0:block_rows]
    scores = (
        jnp.einsum("qhd,khd->hqk", block_queries, pre_keys, preferred_element_type=jnp.float32)
        * score_scale
    )
    same_var = variates[0:block_rows, None] == variates[None, :]
    scores = scores + jnp.where(same_var[None], bias_same[:, None, None], bias_diff[:, None, None])
    allowed = (keep_mask[None, :] == 1) | (
        jnp.arange(0, block_rows)[:, None] == jnp.arange(pre_len)[None, :]
    )
    exp_scores = jnp.where(allowed[None], jnp.exp(scores), 0.0)
    weights_bf = (exp_scores / jnp.sum(exp_scores, axis=2, keepdims=True)).astype(jnp.bfloat16)
    outputs = jnp.einsum(
        "hqk,khd->qhd", weights_bf, pre_values, preferred_element_type=jnp.float32
    ).astype(jnp.bfloat16)
    prefill_out = outputs.reshape(pre_len, local_width)
    peer_count = lax.axis_size("col")
    slot_count = max(2, (dec_count + peer_count - 1) // peer_count)
    holder = dec_holder[:, 0]
    onehot = (holder[:, None] == jnp.arange(peer_count)[None, :]).astype(jnp.int32)
    slot_rank = jnp.sum((jnp.cumsum(onehot, axis=0) - onehot) * onehot, axis=1)
    target = holder * slot_count + slot_rank
    payload = jnp.concatenate(
        [
            query_rot[pre_len:].reshape(dec_count, local_width),
            key_rot[pre_len:].reshape(dec_count, local_width),
            value_bf[pre_len:].reshape(dec_count, local_width),
        ],
        axis=1,
    )
    int_facts = jnp.concatenate([dec_table, dec_len[:, None], dec_variate[:, None]], axis=1)
    send_float = (
        jnp.zeros((peer_count * slot_count, 3 * local_width), jnp.bfloat16).at[target].set(payload)
    )
    send_int = (
        jnp.zeros((peer_count * slot_count, page_count + 2), jnp.int32).at[target].set(int_facts)
    )
    send_float = send_float.reshape(peer_count, slot_count, 3 * local_width)
    send_int = send_int.reshape(peer_count, slot_count, page_count + 2)
    floats = lax.all_to_all(send_float, "col", split_axis=0, concat_axis=0, tiled=True)
    int_part = lax.all_to_all(send_int, "col", split_axis=0, concat_axis=0, tiled=True)
    group_count = floats.shape[0]
    item_count = floats.shape[1]
    flat_floats = floats.reshape(group_count * item_count, floats.shape[2])
    flat_ints = int_part.reshape(group_count * item_count, int_part.shape[2])
    batch_slots = min(16, group_count * item_count)
    slot_out, slot_tail = lax.map(attend_slot, (flat_floats, flat_ints), batch_size=batch_slots)
    slot_out = slot_out.reshape(group_count, item_count, local_width)
    slot_tail = slot_tail.reshape(group_count, item_count, 2, page_size, local_width)
    back_out = lax.all_to_all(
        as_sent(slot_out), "col", split_axis=0, concat_axis=0, tiled=True
    ).astype(slot_out.dtype)
    back_tail = lax.all_to_all(
        as_sent(slot_tail), "col", split_axis=0, concat_axis=0, tiled=True
    ).astype(slot_tail.dtype)
    decode_out = back_out.reshape(peer_count * slot_count, local_width)[target]
    tails = back_tail.reshape(peer_count * slot_count, 2, page_size, local_width)[target]
    decode_out, tail_pages = (decode_out, tails)
    all_attended = jnp.concatenate([prefill_out, decode_out], axis=0)
    partial_out = jnp.dot(
        all_attended,
        lax.all_gather(w_o, "col", axis=1, tiled=True),
        preferred_element_type=jnp.float32,
    )
    share_start = lax.axis_index("row") * local_width
    attn_total = lax.psum(partial_out.astype(jnp.bfloat16), "row").astype(jnp.float32)
    resid_full = gathered_input.astype(jnp.float32) + attn_total
    ffn_input = norm_rows(resid_full, norm2).astype(jnp.bfloat16)
    resid_share = lax.dynamic_slice_in_dim(resid_full, share_start, local_width, 1)
    zero_hidden = jnp.zeros((row_count, w_gate.shape[1]), jnp.float32)
    pieces = (
        lax.all_gather(w_gate, "col", axis=0, tiled=True),
        lax.all_gather(w_up, "col", axis=0, tiled=True),
    )
    columns = lax.slice_in_dim(ffn_input, 0, pieces[0].shape[0], axis=1)
    gate_proj = zero_hidden + jnp.dot(columns, pieces[0], preferred_element_type=jnp.float32)
    up_proj = zero_hidden + jnp.dot(columns, pieces[1], preferred_element_type=jnp.float32)
    hidden_units = (jax.nn.silu(gate_proj) * up_proj).astype(jnp.bfloat16)
    partial_ffn = jnp.dot(
        hidden_units,
        lax.all_gather(w_down, "col", axis=1, tiled=True),
        preferred_element_type=jnp.float32,
    )
    ffn_share = lax.psum_scatter(
        partial_ffn.astype(jnp.bfloat16), "row", scatter_dimension=1, tiled=True
    ).astype(jnp.float32)
    hidden = (resid_share + ffn_share).astype(jnp.bfloat16)
    prefill_pages = jnp.stack(
        [
            key_rot[:pre_len].reshape(pre_len // page_size, page_size, local_width),
            value_bf[:pre_len].reshape(pre_len // page_size, page_size, local_width),
        ],
        axis=1,
    )
    return (hidden, prefill_pages, tail_pages)


def solution(mesh):
    placed = (
        P("col", "row"),
        P("col", "row"),
        P("col", "row"),
        P("col", "row"),
        P("row", "col"),
        P("col", "row"),
        P("col", "row"),
        P("row", "col"),
        P(),
        P(),
        P("row"),
        P("row"),
        P("row"),
        P("row"),
        P("col", None),
        P("col", None),
        P("col"),
        P("col"),
        P("col", None),
        P("col", None),
        P("col", None, None, "row"),
        P("col", None),
    )
    return jax.shard_map(
        on_device,
        mesh=mesh,
        in_specs=placed,
        out_specs=(P("col", "row"), P("col", None, None, "row"), P("col", None, None, "row")),
        check_vma=False,
    )
```

profile of v0, /device:TPU:8, one launch (start us, length us, event | category | flops | bytes accessed | tf_op | source)
XLA Modules:
  0.0 774.8 jit_solution(16630199738598560226)
XLA Ops:
  15.8 51.9 %all_gather.27 = bf16[1024,128]{1,0:T(8,128)(2,1)S(1)} all-gather(bf16[32,128]{1,0:T(8,128)(2,1)} %param.26), channel_id=1, replica_groups=mesh['row'=8,'col'=32] {'col'}, dimensions={0}, use_global_device_ids=true | all-gather | bytes 270336 | tf_op jit(solution)/shard_map/all_gather | solution.py:78
  67.7 47.2 %all_gather.26 = bf16[1024,128]{1,0:T(8,128)(2,1)S(1)} all-gather(bf16[32,128]{1,0:T(8,128)(2,1)} %param.25), channel_id=1, replica_groups=mesh['row'=8,'col'=32] {'col'}, dimensions={0}, use_global_device_ids=true | all-gather | bytes 270336 | tf_op jit(solution)/shard_map/all_gather | solution.py:77
  114.9 47.7 %all_gather.25 = bf16[1024,128]{1,0:T(8,128)(2,1)S(1)} all-gather(bf16[32,128]{1,0:T(8,128)(2,1)} %param.27), channel_id=1, replica_groups=mesh['row'=8,'col'=32] {'col'}, dimensions={0}, use_global_device_ids=true | all-gather | bytes 270336 | tf_op jit(solution)/shard_map/all_gather | solution.py:79
  162.6 51.4 %all_gather.28 = bf16[128,1024]{0,1:T(8,128)(2,1)} all-gather(bf16[128,32]{0,1:T(8,128)(2,1)} %param.28), channel_id=1, replica_groups=mesh['row'=8,'col'=32] {'col'}, dimensions={1}, use_global_device_ids=true | all-gather | bytes 270336 | tf_op jit(solution)/shard_map/all_gather | solution.py:207
  223.5 7.1 all-to-all-start.1
  230.6 8.7 %all-to-all-done.1 = bf16[32,2,384]{2,1,0:T(2,128)(2,1)S(1)} async-done(((bf16[32,2,384]{2,1,0:T(2,128)(2,1)}), bf16[32,2,384]{2,1,0:T(2,128)(2,1)S(1)}, u32[]{:S(2)}, u32[]{:S(2)}) %all-to-all-start.1) | async-done | bytes 49184 | tf_op jit(solution)/shard_map/all_to_all | solution.py:185
  253.0 209.6 %while.14 = (s32[]{:T(128)}, bf16[4,16,128]{2,1,0:T(8,128)(2,1)}, bf16[4,16,2,128,128]{4,3,2,1,0:T(8,128)(2,1)}, s32[4,16,10]{2,1,0:T(8,128)S(1)}, bf16[4,16,384...) while((s32[]{:T(128)}, bf16[4,16,128]{2,1,0:T(8,128)(2,1)}, ...), condition=%wide.region_13.14_spmd, body=%wide.region_10.13_spmd.sunk | while | flops 9330754 | bytes 80879120 | solution.py:192
  273.3 7.3 squeeze.36
  284.3 6.7 copy.137
  291.0 7.3 squeeze.35
  325.7 7.3 squeeze.36
  343.5 7.3 squeeze.35
  378.1 7.3 squeeze.36
  389.1 6.7 copy.137
  395.8 7.3 squeeze.35
  430.4 7.3 squeeze.36
  448.1 7.3 squeeze.35
  470.4 6.9 all-to-all-done.2
  480.2 6.8 all-to-all-start.3
  488.4 58.4 %all-reduce.2.cloned.1.call-done = bf16[528,1024]{1,0:T(8,128)(2,1)} async-done(((bf16[528,1024]{1,0:T(8,128)(2,1)}), bf16[528,1024]{1,0:T(8,128)(2,1)}) %all-reduce.2.cloned.1.call-update) | async-done | bytes 1081360 | tf_op jit(solution)/shard_map/psum | solution.py:211
  548.5 19.2 %all-gather.7.cloned.1.call-done = bf16[1024,512]{1,0:T(8,128)(2,1)} async-done(((bf16[32,512]{1,0:T(8,128)(2,1)}), bf16[1024,512]{1,0:T(8,128)(2,1)}) %all-gather.7.cloned.1.call-update) | async-done | bytes 1048592 | tf_op jit(solution)/shard_map/all_gather | solution.py:217
  571.0 73.5 %all-gather.11.cloned.1.call-done = bf16[512,1024]{0,1:T(8,128)(2,1)} async-done(((bf16[512,32]{0,1:T(8,128)(2,1)}), bf16[512,1024]{0,1:T(8,128)(2,1)}) %all-gather.11.cloned.1.call-update) | async-done | bytes 1048592 | tf_op jit(solution)/shard_map/all_gather | solution.py:226
  644.5 76.8 %all-gather.9.cloned.1.call-done = bf16[1024,512]{1,0:T(8,128)(2,1)} async-done(((bf16[32,512]{1,0:T(8,128)(2,1)}), bf16[1024,512]{1,0:T(8,128)(2,1)}) %all-gather.9.cloned.1.call-update) | async-done | bytes 1048592 | tf_op jit(solution)/shard_map/all_gather | solution.py:218
  729.3 32.6 %reduce-scatter.4.cloned.1.call-done = bf16[128,528]{1,0:T(8,128)(2,1)} async-done(((bf16[1024,528]{1,0:T(8,128)(2,1)}), bf16[128,528]{1,0:T(8,128)(2,1)}) %reduce-scatter.4.cloned.1.call-update) | async-done | bytes 135184
  (249 shorter events, 198.7 us)
Async XLA Ops:
  8.0 210.7 %copy-start.7 = (f32[1024]{0:T(1024)S(1)}, f32[1024]{0:T(1024)}, u32[]{:S(2)}) copy-start(f32[1024]{0:T(1024)} %param.32) | copy-start | bytes 12292
  8.0 209.0 %all-gather.5.cloned.1.call-start = ((), (), s32[]{:S(2)}) async-start(), calls=%async_computation.5 | async-start | bytes 1216512 | tf_op jit(solution)/shard_map/all_gather | solution.py:74
  217.0 3.5 copy-start.2
  221.4 22.9 %copy-start.5 = (f32[2]{0:T(128)S(1)}, f32[2]{0:T(128)}, u32[]{:S(2)}) copy-start(f32[2]{0:T(128)} %param.36) | copy-start | bytes 28
  221.4 22.9 %copy-start.6 = (f32[2]{0:T(128)S(1)}, f32[2]{0:T(128)}, u32[]{:S(2)}) copy-start(f32[2]{0:T(128)} %param.37) | copy-start | bytes 28
  223.5 15.8 %all-to-all-start.1 = ((bf16[32,2,384]{2,1,0:T(2,128)(2,1)}), bf16[32,2,384]{2,1,0:T(2,128)(2,1)S(1)}, u32[]{:S(2)}, u32[]{:S(2)}) async-start(bf16[32,2,384]{2,1,0:T(2,128)(2,1)} %reshape.400), calls=%async_computation.1 | async-start | bytes 98304 | tf_op jit(solution)/shard_map/all_to_all | solution.py:185
  239.3 13.7 %all-to-all-start = ((s32[32,2,10]{2,1,0:T(2,128)}), s32[32,2,10]{2,1,0:T(2,128)S(1)}, u32[]{:S(2)}, u32[]{:S(2)}) async-start(s32[32,2,10]{2,1,0:T(2,128)} %bitcast.30), calls=%async_computation | async-start | bytes 65536 | tf_op jit(solution)/shard_map/all_to_all | solution.py:186
  244.3 8.7 %copy-start = (bf16[32,2,128,128]{3,2,1,0:T(8,128)(2,1)S(1)}, bf16[32,2,128,128]{3,2,1,0:T(8,128)(2,1)}, u32[]{:S(2)}) copy-start(bf16[32,2,128,128]{3,2,1,0:T(8,128)(2,1)} %param.44) | copy-start | bytes 6291460
  244.3 8.7 %copy-start.1 = (s32[32,128]{1,0:T(8,128)S(1)}, s32[32,128]{1,0:T(8,128)}, u32[]{:S(2)}) copy-start(s32[32,128]{1,0:T(8,128)} %param.45) | copy-start | bytes 49156
  462.5 14.8 %all-to-all-start.2 = ((bf16[32,2,128]{2,1,0:T(2,128)(2,1)}), bf16[32,2,128]{2,1,0:T(2,128)(2,1)S(1)}, u32[]{:S(2)}, u32[]{:S(2)}) async-start(bf16[32,2,128]{2,1,0:T(2,128)(2,1)} %bitcast.34), calls=%async_computation.2 | async-start | bytes 32768 | tf_op jit(solution)/shard_map/all_to_all | solution.py:195
  467.6 79.2 %all-reduce.2.cloned.1.call-start = ((), (), s32[]{:S(2)}) async-start(), calls=%async_computation.6 | async-start | bytes 2162688 | tf_op jit(solution)/shard_map/psum | solution.py:211
  467.7 10.4 %copy-start.4 = (bf16[128,1024]{0,1:T(8,128)(2,1)S(1)}, bf16[128,1024]{0,1:T(8,128)(2,1)}, u32[]{:S(2)}) copy-start(bf16[128,1024]{0,1:T(8,128)(2,1)} %all_gather.28) | copy-start | bytes 786436
  479.6 88.1 %all-gather.7.cloned.1.call-start = ((), (), s32[]{:S(2)}) async-start(), calls=%async_computation.7 | async-start | bytes 1081344 | tf_op jit(solution)/shard_map/all_gather | solution.py:217
  480.2 66.7 %copy-start.3 = (bf16[528,1024]{1,0:T(8,128)(2,1)S(1)}, bf16[528,1024]{1,0:T(8,128)(2,1)}, u32[]{:S(2)}) copy-start(bf16[528,1024]{1,0:T(8,128)(2,1)} %all-gather.5.cloned.1.call-done) | copy-start | bytes 3244036
  480.2 283.5 %all-to-all-start.3 = ((bf16[32,2,2,128,128]{4,3,2,1,0:T(8,128)(2,1)}), bf16[32,2,2,128,128]{4,3,2,1,0:T(8,128)(2,1)}, u32[]{:S(2)}, u32[]{:S(2)}) async-start(bf16[32,2,2,128,128]{4,3,2,1,0:T(8,128)(2,1)} %bitcast.142), calls=%async_computation.3 | async-start | bytes 8388608 | tf_op jit(solution)/shard_map/all_to_all | solution.py:198
  487.0 157.5 %all-gather.11.cloned.1.call-start = ((), (), s32[]{:S(2)}) async-start(), calls=%async_computation.9 | async-start | bytes 1081344 | tf_op jit(solution)/shard_map/all_gather | solution.py:226
  487.6 233.7 %all-gather.9.cloned.1.call-start = ((), (), s32[]{:S(2)}) async-start(), calls=%async_computation.8 | async-start | bytes 1081344 | tf_op jit(solution)/shard_map/all_gather | solution.py:218
  488.1 79.6 %copy-start.8 = (f32[1024]{0:T(1024)S(1)}, f32[1024]{0:T(1024)}, u32[]{:S(2)}) copy-start(f32[1024]{0:T(1024)} %param.33) | copy-start | bytes 12292
  488.1 273.8 %reduce-scatter.4.cloned.1.call-start = ((), (), s32[]{:S(2)}) async-start(), calls=%async_computation.10 | async-start | bytes 1474560
Sparse Core Ops, SparseCore 0:
  10.7 28.8 all-gather.4
  479.7 67.0 all-reduce.1
  728.5 33.3 reduce-scatter.3
Sparse Core Ops, SparseCore 1:
  483.0 84.7 all-gather.6
  570.5 73.9 all-gather.10
  647.3 74.0 all-gather.8
where the time goes:
time: 778 us; the launch traced here: 775 us
  waiting for transfers between devices  284 us (37%)
  blocking collectives  198 us (25%)
  local copies, waits for them, and re-layouts  189 us (24%)
  matrix products  42.3 us (5%)
  starting transfers between devices  24.4 us (3%)
  other arithmetic  21.1 us (3%)
  between operations  15.7 us (2%)
    all_gather x1, waiting for transfers between devices, on_device(): lax.all_gather(w_up, 'col', axis=0, tiled=True)  76.8 us
    all_gather x1, waiting for transfers between devices, on_device(): lax.all_gather(w_down, 'col', axis=1, tiled=True)  73.5 us
    psum x1, waiting for transfers between devices, on_device(): lax.psum(partial_out.astype(jnp.bfloat16), 'row').astype(jnp.float32)  58.4 us
    while x8, local copies, waits for them, and re-layouts  53.9 us
    all_gather x1, blocking collectives, on_device(): lax.all_gather(w_k, 'col', axis=0, tiled=True)  51.9 us
    all_gather x1, blocking collectives, on_device(): lax.all_gather(w_o, 'col', axis=1, tiled=True)  51.4 us
    all_gather x1, blocking collectives, on_device(): lax.all_gather(w_v, 'col', axis=0, tiled=True)  47.7 us
    all_gather x1, blocking collectives, on_device(): lax.all_gather(w_q, 'col', axis=0, tiled=True)  47.2 us
  transfers between devices with their start and end apart: 10, of which 8 were waited for; matrix products, arithmetic and copies ran while one was open for 4% of the time, Pallas kernels for 0%

commit v1 on v0

--- a/solution.py
+++ b/solution.py
@@ -1,3 +1,4 @@
+import functools
 import jax
 import jax.numpy as jnp
 from jax import lax
@@ -5,6 +6,13 @@
 
 HD = 64
 eps = 1e-05
+
+
+def _settle_sources_all(point, axis_name):
+    return lax.all_gather(point, axis_name=axis_name).sum(axis=0)
+
+
+_fit_racks = functools.partial(_settle_sources_all, axis_name="row")
 
 
 def as_sent(array):
@@ -208,7 +216,7 @@
         preferred_element_type=jnp.float32,
     )
     share_start = lax.axis_index("row") * local_width
-    attn_total = lax.psum(partial_out.astype(jnp.bfloat16), "row").astype(jnp.float32)
+    attn_total = _fit_racks(partial_out.astype(jnp.bfloat16)).astype(jnp.float32)
     resid_full = gathered_input.astype(jnp.float32) + attn_total
     ffn_input = norm_rows(resid_full, norm2).astype(jnp.bfloat16)
     resid_share = lax.dynamic_slice_in_dim(resid_full, share_start, local_width, 1)

time: 778 us -> 814 us (1.046)
  waiting for transfers between devices: 284 us -> 315 us
    psum x1 -> x0, waiting for transfers between devices: 58.4 us -> none  [on_device(): lax.psum(partial_out.astype(jnp.bfloat16), 'row').astype(jnp.float32)]
    all_gather x1, waiting for transfers between devices: 19.2 us -> 70.4 us  [on_device(): lax.all_gather(w_gate, 'col', axis=0, tiled=True)]
    all_gather x0 -> x1, waiting for transfers between devices: none -> 42.5 us  [_settle_sources_all(): return lax.all_gather(point, axis_name=axis_name).sum(axis=0)]
  transfers between devices with their start and end apart: 10 -> 10, of which waited for: 8 -> 8; matrix products, arithmetic and copies ran while one was open for 4% -> 5% of each run, Pallas kernels for 0% -> 0%
where the time goes in v1:
time: 814 us; the launch traced here: 811 us
  waiting for transfers between devices  315 us (39%)
  blocking collectives  198 us (24%)
  local copies, waits for them, and re-layouts  189 us (23%)
  matrix products  41.6 us (5%)
  other arithmetic  28 us (3%)
  starting transfers between devices  24.5 us (3%)
  between operations  14.4 us (2%)
    all_gather x1, waiting for transfers between devices, on_device(): lax.all_gather(w_down, 'col', axis=1, tiled=True)  76.3 us
    all_gather x1, waiting for transfers between devices, on_device(): lax.all_gather(w_up, 'col', axis=0, tiled=True)  73.3 us
    all_gather x1, waiting for transfers between devices, on_device(): lax.all_gather(w_gate, 'col', axis=0, tiled=True)  70.4 us
    while x8, local copies, waits for them, and re-layouts  53.9 us
    all_gather x1, blocking collectives, on_device(): lax.all_gather(w_k, 'col', axis=0, tiled=True)  51.9 us
    all_gather x1, blocking collectives, on_device(): lax.all_gather(w_o, 'col', axis=1, tiled=True)  51.3 us
    all_gather x1, blocking collectives, on_device(): lax.all_gather(w_v, 'col', axis=0, tiled=True)  47.7 us
    all_gather x1, blocking collectives, on_device(): lax.all_gather(w_q, 'col', axis=0, tiled=True)  47.2 us
  transfers between devices with their start and end apart: 10, of which 8 were waited for; matrix products, arithmetic and copies ran while one was open for 5% of the time, Pallas kernels for 0%

profile of v1, /device:TPU:8, one launch (start us, length us, event | category | flops | bytes accessed | tf_op | source)
XLA Modules:
  0.0 810.7 jit_solution(4915879611112641805)
XLA Ops:
  15.0 51.9 %all_gather.33 = bf16[1024,128]{1,0:T(8,128)(2,1)S(1)} all-gather(bf16[32,128]{1,0:T(8,128)(2,1)} %param.26), channel_id=1, replica_groups=mesh['row'=8,'col'=32] {'col'}, dimensions={0}, use_global_device_ids=true | all-gather | bytes 270336 | tf_op jit(solution)/shard_map/all_gather | solution.py:86
  66.9 47.2 %all_gather.32 = bf16[1024,128]{1,0:T(8,128)(2,1)S(1)} all-gather(bf16[32,128]{1,0:T(8,128)(2,1)} %param.25), channel_id=1, replica_groups=mesh['row'=8,'col'=32] {'col'}, dimensions={0}, use_global_device_ids=true | all-gather | bytes 270336 | tf_op jit(solution)/shard_map/all_gather | solution.py:85
  114.1 47.7 %all_gather.31 = bf16[1024,128]{1,0:T(8,128)(2,1)S(1)} all-gather(bf16[32,128]{1,0:T(8,128)(2,1)} %param.27), channel_id=1, replica_groups=mesh['row'=8,'col'=32] {'col'}, dimensions={0}, use_global_device_ids=true | all-gather | bytes 270336 | tf_op jit(solution)/shard_map/all_gather | solution.py:87
  161.7 51.3 %all_gather.34 = bf16[128,1024]{0,1:T(8,128)(2,1)} all-gather(bf16[128,32]{0,1:T(8,128)(2,1)} %param.28), channel_id=1, replica_groups=mesh['row'=8,'col'=32] {'col'}, dimensions={1}, use_global_device_ids=true | all-gather | bytes 270336 | tf_op jit(solution)/shard_map/all_gather | solution.py:215
  222.5 7.3 all-to-all-start.1
  229.9 8.7 %all-to-all-done.1 = bf16[32,2,384]{2,1,0:T(2,128)(2,1)S(1)} async-done(((bf16[32,2,384]{2,1,0:T(2,128)(2,1)}), bf16[32,2,384]{2,1,0:T(2,128)(2,1)S(1)}, u32[]{:S(2)}, u32[]{:S(2)}) %all-to-all-start.1) | async-done | bytes 49184 | tf_op jit(solution)/shard_map/all_to_all | solution.py:193
  252.2 209.7 %while.14 = (s32[]{:T(128)}, bf16[4,16,128]{2,1,0:T(8,128)(2,1)}, bf16[4,16,2,128,128]{4,3,2,1,0:T(8,128)(2,1)}, s32[4,16,10]{2,1,0:T(8,128)S(1)}, bf16[4,16,384...) while((s32[]{:T(128)}, bf16[4,16,128]{2,1,0:T(8,128)(2,1)}, ...), condition=%wide.region_13.14_spmd, body=%wide.region_10.13_spmd.sunk | while | flops 9330754 | bytes 80879120 | solution.py:200
  272.6 7.3 squeeze.36
  283.6 6.7 copy.137
  290.3 7.3 squeeze.35
  325.0 7.3 squeeze.36
  336.0 6.7 copy.137
  342.8 7.3 squeeze.35
  377.4 7.3 squeeze.36
  388.4 6.7 copy.137
  395.1 7.3 squeeze.35
  429.8 7.3 squeeze.36
  447.5 7.3 squeeze.35
  469.8 6.9 all-to-all-done.2
  487.7 42.5 %all-gather.15.cloned.1.call-done = bf16[4224,1024]{1,0:T(8,128)(2,1)} async-done(((bf16[528,1024]{1,0:T(8,128)(2,1)}), bf16[4224,1024]{1,0:T(8,128)(2,1)}) %all-gather.15.cloned.1.call-update) | async-done | bytes 8650768 | tf_op jit(solution)/shard_map/all_gather | solution.py:12
  537.9 70.4 %all-gather.9.cloned.1.call-done = bf16[1024,512]{1,0:T(8,128)(2,1)} async-done(((bf16[32,512]{1,0:T(8,128)(2,1)}), bf16[1024,512]{1,0:T(8,128)(2,1)}) %all-gather.9.cloned.1.call-update) | async-done | bytes 1048592 | tf_op jit(solution)/shard_map/all_gather | solution.py:225
  611.3 73.3 %all-gather.11.cloned.1.call-done = bf16[1024,512]{1,0:T(8,128)(2,1)} async-done(((bf16[32,512]{1,0:T(8,128)(2,1)}), bf16[1024,512]{1,0:T(8,128)(2,1)}) %all-gather.11.cloned.1.call-update) | async-done | bytes 1048592 | tf_op jit(solution)/shard_map/all_gather | solution.py:226
  684.6 76.3 %all-gather.13.cloned.1.call-done = bf16[512,1024]{0,1:T(8,128)(2,1)} async-done(((bf16[512,32]{0,1:T(8,128)(2,1)}), bf16[512,1024]{0,1:T(8,128)(2,1)}) %all-gather.13.cloned.1.call-update) | async-done | bytes 1048592 | tf_op jit(solution)/shard_map/all_gather | solution.py:234
  772.4 28.8 %reduce-scatter.4.cloned.1.call-done = bf16[128,528]{1,0:T(8,128)(2,1)} async-done(((bf16[1024,528]{1,0:T(8,128)(2,1)}), bf16[128,528]{1,0:T(8,128)(2,1)}) %reduce-scatter.4.cloned.1.call-update) | async-done | bytes 135184
  (250 shorter events, 205.1 us)
Async XLA Ops:
  7.2 210.5 %copy-start.7 = (f32[1024]{0:T(1024)S(1)}, f32[1024]{0:T(1024)}, u32[]{:S(2)}) copy-start(f32[1024]{0:T(1024)} %param.32) | copy-start | bytes 12292
  7.2 208.9 %all-gather.7.cloned.1.call-start = ((), (), s32[]{:S(2)}) async-start(), calls=%async_computation.5 | async-start | bytes 1216512 | tf_op jit(solution)/shard_map/all_gather | solution.py:82
  216.0 3.5 copy-start.2
  220.4 23.1 %copy-start.5 = (f32[2]{0:T(128)S(1)}, f32[2]{0:T(128)}, u32[]{:S(2)}) copy-start(f32[2]{0:T(128)} %param.36) | copy-start | bytes 28
  220.4 23.1 %copy-start.6 = (f32[2]{0:T(128)S(1)}, f32[2]{0:T(128)}, u32[]{:S(2)}) copy-start(f32[2]{0:T(128)} %param.37) | copy-start | bytes 28
  222.5 16.0 %all-to-all-start.1 = ((bf16[32,2,384]{2,1,0:T(2,128)(2,1)}), bf16[32,2,384]{2,1,0:T(2,128)(2,1)S(1)}, u32[]{:S(2)}, u32[]{:S(2)}) async-start(bf16[32,2,384]{2,1,0:T(2,128)(2,1)} %reshape.400), calls=%async_computation.1 | async-start | bytes 98304 | tf_op jit(solution)/shard_map/all_to_all | solution.py:193
  238.5 13.7 %all-to-all-start = ((s32[32,2,10]{2,1,0:T(2,128)}), s32[32,2,10]{2,1,0:T(2,128)S(1)}, u32[]{:S(2)}, u32[]{:S(2)}) async-start(s32[32,2,10]{2,1,0:T(2,128)} %bitcast.30), calls=%async_computation | async-start | bytes 65536 | tf_op jit(solution)/shard_map/all_to_all | solution.py:194
  243.5 8.7 %copy-start = (bf16[32,2,128,128]{3,2,1,0:T(8,128)(2,1)S(1)}, bf16[32,2,128,128]{3,2,1,0:T(8,128)(2,1)}, u32[]{:S(2)}) copy-start(bf16[32,2,128,128]{3,2,1,0:T(8,128)(2,1)} %param.44) | copy-start | bytes 6291460
  243.5 8.7 %copy-start.1 = (s32[32,128]{1,0:T(8,128)S(1)}, s32[32,128]{1,0:T(8,128)}, u32[]{:S(2)}) copy-start(s32[32,128]{1,0:T(8,128)} %param.45) | copy-start | bytes 49156
  461.9 14.8 %all-to-all-start.2 = ((bf16[32,2,128]{2,1,0:T(2,128)(2,1)}), bf16[32,2,128]{2,1,0:T(2,128)(2,1)S(1)}, u32[]{:S(2)}, u32[]{:S(2)}) async-start(bf16[32,2,128]{2,1,0:T(2,128)(2,1)} %bitcast.34), calls=%async_computation.2 | async-start | bytes 32768 | tf_op jit(solution)/shard_map/all_to_all | solution.py:203
  467.0 63.2 %all-gather.15.cloned.1.call-start = ((), (), s32[]{:S(2)}) async-start(), calls=%async_computation.9 | async-start | bytes 9732096 | tf_op jit(solution)/shard_map/all_gather | solution.py:12
  467.1 10.3 %copy-start.4 = (bf16[128,1024]{0,1:T(8,128)(2,1)S(1)}, bf16[128,1024]{0,1:T(8,128)(2,1)}, u32[]{:S(2)}) copy-start(bf16[128,1024]{0,1:T(8,128)(2,1)} %all_gather.34) | copy-start | bytes 786436
  478.9 129.4 %all-gather.9.cloned.1.call-start = ((), (), s32[]{:S(2)}) async-start(), calls=%async_computation.6 | async-start | bytes 1081344 | tf_op jit(solution)/shard_map/all_gather | solution.py:225
  479.7 288.9 %all-to-all-start.3 = ((bf16[32,2,2,128,128]{4,3,2,1,0:T(8,128)(2,1)}), bf16[32,2,2,128,128]{4,3,2,1,0:T(8,128)(2,1)}, u32[]{:S(2)}, u32[]{:S(2)}) async-start(bf16[32,2,2,128,128]{4,3,2,1,0:T(8,128)(2,1)} %bitcast.144), calls=%async_computation.3 | async-start | bytes 8388608 | tf_op jit(solution)/shard_map/all_to_all | solution.py:206
  486.3 198.3 %all-gather.11.cloned.1.call-start = ((), (), s32[]{:S(2)}) async-start(), calls=%async_computation.7 | async-start | bytes 1081344 | tf_op jit(solution)/shard_map/all_gather | solution.py:226
  486.9 274.0 %all-gather.13.cloned.1.call-start = ((), (), s32[]{:S(2)}) async-start(), calls=%async_computation.8 | async-start | bytes 1081344 | tf_op jit(solution)/shard_map/all_gather | solution.py:234
  487.5 313.6 %reduce-scatter.4.cloned.1.call-start = ((), (), s32[]{:S(2)}) async-start(), calls=%async_computation.10 | async-start | bytes 1474560
  530.2 5.9 copy-start.3
  536.2 72.1 %copy-start.8 = (f32[1024]{0:T(1024)S(1)}, f32[1024]{0:T(1024)}, u32[]{:S(2)}) copy-start(f32[1024]{0:T(1024)} %param.33) | copy-start | bytes 12292
Sparse Core Ops, SparseCore 0:
  9.8 28.8 all-gather.6
  479.0 51.1 all-gather.14
  532.8 75.4 all-gather.8
  610.7 73.8 all-gather.10
  687.0 73.8 all-gather.12
  767.7 33.3 reduce-scatter.3
